TPU v7x, 128 devices: a whole 4x4x4 slice. The times are simulated.
128 devices in a mesh: wide: 16 (over x, z_lo, core), narrow: 8 (over z_hi, y).
Axes of the slice: x: 4, y: 4, z: 4 (z_hi: 2, z_lo: 2; z = z_hi * 2 + z_lo), core: 2. Of those that a mesh axis runs over, the one named last changes fastest.
Arguments:
- amplitudes: float32 [2, 16, 8, 16, 256, 256], P(None, 'wide', 'narrow'), may hold values from -6 to 6
- low_gate: float32 [2, 256, 256], replicated, may hold values from -0.25 to 0.25
- mid_gate: float32 [2, 256, 256], replicated, may hold values from -0.25 to 0.25
- pair_gates: float32 [3, 2, 4, 4], replicated, may hold values from -2 to 2
Outputs:
- remapped: float32 [2, 16, 8, 16, 256, 256], P(None, 'wide', 'narrow')
All inputs are finite; a program needn't handle non-finite values.
Results may differ from a plain program's by a relative error of at most 0.00007.
Values sent between devices are 32-bit elements; how exact they have to be, the bound alone decides.
No kernel may reach another device: no remote copies, remote signals or barrier semaphores. Data moves between devices by JAX's collectives and lax.ppermute only.
A program may use at most 128 MiB of HBM per device.

v0:
```python
import jax
import jax.numpy as jnp
from jax import lax
from jax.sharding import PartitionSpec as P

highest = lax.Precision.HIGHEST


def swapped(x, axis, bit):
    return lax.ppermute(x, axis, [(i, i ^ 1 << bit) for i in range(lax.axis_size(axis))])


def apply_merged(amplitudes, low_gate, mid_gate):
    real_part, imag_part = (amplitudes[0], amplitudes[1])
    low_real, low_imag = (low_gate[0], low_gate[1])
    first_real = jnp.einsum("abhml,il->abhmi", real_part, low_real, precision=highest) - jnp.einsum(
        "abhml,il->abhmi", imag_part, low_imag, precision=highest
    )
    first_imag = jnp.einsum("abhml,il->abhmi", real_part, low_imag, precision=highest) + jnp.einsum(
        "abhml,il->abhmi", imag_part, low_real, precision=highest
    )
    mid_real, mid_imag = (mid_gate[0], mid_gate[1])
    second_real = jnp.einsum(
        "abhml,im->abhil", first_real, mid_real, precision=highest
    ) - jnp.einsum("abhml,im->abhil", first_imag, mid_imag, precision=highest)
    second_imag = jnp.einsum(
        "abhml,im->abhil", first_real, mid_imag, precision=highest
    ) + jnp.einsum("abhml,im->abhil", first_imag, mid_real, precision=highest)
    return jnp.stack([second_real, second_imag])


def partner_gate(state, other, gate, mine, half_bit):
    rows = lax.dynamic_slice_in_dim(gate, 2 * mine, 2, 1)
    own_cols = lax.dynamic_slice_in_dim(rows, 2 * mine, 2, 2)
    far_cols = lax.dynamic_slice_in_dim(rows, 2 - 2 * mine, 2, 2)
    shape = state.shape
    split_shape = shape[:3] + (shape[3] >> half_bit + 1, 2, 1 << half_bit) + shape[4:]
    own_split = state.reshape(split_shape)
    far_split = other.reshape(split_shape)
    outputs = []
    for target in range(2):
        total_real = jnp.zeros(own_split[0, :, :, :, 0].shape, jnp.float32)
        total_imag = jnp.zeros(own_split[0, :, :, :, 0].shape, jnp.float32)
        for source in range(2):
            for coeffs, piece in ((own_cols, own_split), (far_cols, far_split)):
                amplitude = piece[:, :, :, :, source]
                coef_real = coeffs[0, target, source]
                coef_imag = coeffs[1, target, source]
                total_real = total_real + coef_real * amplitude[0] - coef_imag * amplitude[1]
                total_imag = total_imag + coef_real * amplitude[1] + coef_imag * amplitude[0]
        outputs.append(jnp.stack([total_real, total_imag]))
    return jnp.stack(outputs, axis=4).reshape(shape)


def narrow_gate(state, gate):
    other = swapped(state, "narrow", 1)
    mine = lax.axis_index("narrow") >> 1 & 1
    return partner_gate(state, other, gate, mine, 0)


def remap_qubits(state):
    return lax.all_to_all(state, "wide", split_axis=4, concat_axis=4, tiled=True)


def body(amplitudes, low_gate, mid_gate, pair_gates):
    state = apply_merged(amplitudes, low_gate, mid_gate)
    wide_index = lax.axis_index("wide")
    other = swapped(state, "wide", 0)
    state = partner_gate(state, other, pair_gates[0], wide_index & 1, 0)
    other = swapped(state, "wide", 2)
    state = partner_gate(state, other, pair_gates[1], wide_index >> 2 & 1, 1)
    state = narrow_gate(state, pair_gates[2])
    state = remap_qubits(state)
    return state


def solution(mesh):
    in_specs = (P(None, "wide", "narrow", None, None, None), P(), P(), P())
    out_specs = P(None, "wide", "narrow", None, None, None)
    return jax.shard_map(body, mesh=mesh, in_specs=in_specs, out_specs=out_specs, check_vma=False)
```

profile of v0, /device:TPU:1, one launch (start us, length us, event | category | flops | bytes accessed | tf_op | source)
XLA Modules:
  0.0 675.4 jit_solution(6235137157490432231)
XLA Ops:
  0.0 5.5 fusion.2
  5.5 0.0 copy-start.10
  5.5 4.5 fusion
  10.0 3.5 fusion.12
  13.5 6.9 %fusion.42 = f32[16,256,256]{2,1,0:T(8,128)S(1)} fusion(f32[16,256,256]{2,1,0:T(8,128)S(1)} %fusion.12, f32[2,256,256]{2,1,0:T(8,128)S(1)} %copy-done.11), kind=kOutput, calls=%fused_computation.77 | convolution fusion | flops 3221225472 | bytes 8650752 | tf_op jit(solution)/shard_map/abhml,im->abhil/dot_general | solution.py:26
  20.4 7.0 %fusion.46 = f32[16,256,256]{2,1,0:T(8,128)S(1)} fusion(f32[16,256,256]{2,1,0:T(8,128)S(1)} %fusion.12, f32[2,256,256]{2,1,0:T(8,128)S(1)} %copy-done.11), kind=kOutput, calls=%fused_computation.81 | convolution fusion | flops 3221225472 | bytes 8650752 | tf_op jit(solution)/shard_map/abhml,im->abhil/dot_general | solution.py:23
  27.3 3.9 fusion.15
  31.2 7.1 %convolution_add_fusion = f32[16,256,256]{2,1,0:T(8,128)S(1)} fusion(f32[16,256,256]{2,1,0:T(8,128)S(1)} %fusion.42, f32[16,256,256]{2,1,0:T(8,128)S(1)} %fusion.15, f32[2,256,256]{2,1,0:T(8,128)S(1)} %copy-done.11), kind=kOutput, calls=%fused_computation.25 | convolution fusion | flops 3222274048 | bytes 12845056 | tf_op jit(solution)/shard_map/abhml,im->abhil/dot_general | solution.py:28
  38.3 7.2 %convolution_subtract_fusion = f32[16,256,256]{2,1,0:T(8,128)S(1)} fusion(f32[16,256,256]{2,1,0:T(8,128)S(1)} %fusion.46, f32[16,256,256]{2,1,0:T(8,128)S(1)} %fusion.15, f32[2,256,256]{2,1,0:T(8,128)S(1)} %copy-done.11), kind=kOutput, calls=%fused_computation.26 | convolution fusion | flops 3222274048 | bytes 12845056 | tf_op jit(solution)/shard_map/abhml,im->abhil/dot_general | solution.py:25
  45.5 4.3 pad_maximum_fusion
  49.8 0.2 copy-done
  50.0 1.4 collective-permute-start
  51.5 4.6 fusion.62
  56.0 1.9 copy.186
  58.0 4.6 fusion.63
  62.6 2.9 copy.185
  65.5 2.9 copy.182
  68.4 2.9 copy.181
  71.3 0.1 dynamic-slice_bitcast_fusion.3
  71.4 0.7 fusion.70
  72.1 0.7 fusion.69
  72.7 6.9 %fusion.61 = (f32[1,1,1,8,1,1,256,256]{6,7,4,3,0,5,2,1:T(8,128)}, f32[1,1,1,8,1,1,256,256]{6,7,4,3,0,5,2,1:T(8,128)}, f32[1,1,1,8,1,1,256,256]{6,7,4,3,0,5,2,1:T(8,128)}, f32[1,1,1,8,1,1,256,256]{6,7,4,3,0,5,2,1:T(8,128)}) fusion(f32[2,1,1,8,2,1,256,256]{6,7,4,3,0,5,2,1:T(8,128)} %bitcast.33), kind=kLoop, calls=%fused_computation.102 | loop fusion | bytes 16777216 | tf_op jit(solution)/shard_map/slice | solution.py:49
  79.6 2.9 copy.188
  82.5 2.9 copy.187
  85.4 2.9 copy.184
  88.3 2.9 copy.183
  91.2 11.9 %add_subtract_fusion = (f32[1,1,1,8,1,1,256,256]{7,6,3,5,4,2,1,0:T(8,128)S(1)}, f32[1,1,1,8,1,1,256,256]{7,6,3,5,4,2,1,0:T(8,128)S(1)}) fusion(f32[1,1,1,8,1,1,256,256]{7,6,3,5,4,2,1,0:T(8,128)} %copy.188, f32[1,1,1,8,1,1,256,256]{7,6,3,5,4,2,1,0:T(8,128)} %copy.187, f32[1,1,1,8,1,1,256,256]{7,6,3,5,4,2,1,0:T(8,128)S(1)} %copy.186, ...), kind=kLoop, calls=%fused_computation.74 | loop fusion | flops 15728640 | bytes 20971552 | tf_op jit(solution)/shard_map/sub | solution.py:49
  103.2 0.4 maximum_bitcast_fusion.1
  103.7 1.1 copy-done.3
  104.7 0.6 copy-done.4
  105.4 0.6 copy-done.5
  106.0 0.6 copy-done.6
  106.6 6.9 %add_subtract_fusion.1 = (f32[1,1,1,8,1,1,256,256]{7,6,3,5,4,2,1,0:T(8,128)S(1)}, f32[1,1,1,8,1,1,256,256]{7,6,3,5,4,2,1,0:T(8,128)S(1)}) fusion(f32[1,1,1,8,1,1,256,256]{7,6,3,5,4,2,1,0:T(8,128)S(1)} %copy-done.6, f32[1,1,1,8,1,1,256,256]{7,6,3,5,4,2,1,0:T(8,128)S(1)} %copy-done.7, f32[1,1,1,8,1,1,256,256]{7,6,3,5,4,2,1,0:T(8,128)S(1)} %copy.186, ...), kind=kLoop, calls=%fused_computation.76 | loop fusion | flops 15728640 | bytes 20971552 | tf_op jit(solution)/shard_map/sub | solution.py:49
  113.5 0.4 maximum_bitcast_fusion
  113.9 4.0 pad_maximum_fusion.1
  117.9 1.3 collective-permute-start.1
  119.2 0.6 fusion.68
  119.8 0.7 fusion.67
  120.5 3.6 maximum_maximum_fusion
  124.1 4.0 fusion.60
  128.1 172.1 %collective-permute-done.1 = f32[2,1,1,16,256,256]{5,4,3,0,2,1:T(8,128)S(1)} collective-permute-done((f32[2,1,1,16,256,256]{5,4,3,0,2,1:T(8,128)}, f32[2,1,1,16,256,256]{5,4,3,0,2,1:T(8,128)S(1)}, u32[]{:S(2)}, u32[]{:S(2)}) %collective-permute-start.1) | collective-permute-done | bytes 8388640 | tf_op jit(solution)/shard_map/ppermute | solution.py:10
  300.2 6.0 fusion.33
  306.2 6.0 fusion.41
  312.2 6.1 fusion.39
  318.2 6.1 fusion.36
  324.3 0.3 maximum_bitcast_fusion.3
  324.6 0.3 maximum_bitcast_fusion.2
  324.9 0.9 pad_maximum_fusion.2
  325.8 4.0 copy.153
  329.7 3.0 collective-permute-start.2
  332.7 0.1 dynamic-slice_bitcast_fusion.5
  332.8 0.7 fusion.65
  333.5 179.3 %collective-permute-done.2 = f32[2,1,1,16,256,256]{5,4,3,0,2,1:T(8,128)} collective-permute-done((f32[2,1,1,16,256,256]{5,4,3,0,2,1:T(8,128)}, f32[2,1,1,16,256,256]{5,4,3,0,2,1:T(8,128)}, u32[]{:S(2)}, u32[]{:S(2)}) %collective-permute-start.2) | collective-permute-done | bytes 8388640 | tf_op jit(solution)/shard_map/ppermute | solution.py:10
  512.8 11.5 %fusion.18 = f32[1,1,1,8,1,256,256]{6,5,3,4,2,1,0:T(8,128)S(1)} fusion(f32[2,1,1,8,2,1,256,256]{7,6,4,3,0,5,2,1:T(8,128)} %bitcast.92, f32[2,1,1,8,2,1,256,256]{7,6,4,3,0,5,2,1:T(8,128)} %bitcast.97, f32[]{:T(128)} %bitcast.117, f32[]{:T(128)} %bitcast.116, f32[]{:T(128)} %bitcast.114, f32[]{:T(128)} %bitcast.113, f32[]{:T(128)} %bitcast.112, f32[]{:T(128)} %bitcast.111, ...), kind=kLoop, calls=%fused_computation.38 | loop fusion | flops 7864320 | bytes 18874400 | tf_op jit(solution)/shard_map/add | solution.py:50
  524.4 11.3 %fusion.32 = f32[1,1,1,8,1,256,256]{6,5,3,4,2,1,0:T(8,128)S(1)} fusion(f32[2,1,1,8,2,1,256,256]{7,6,4,3,0,5,2,1:T(8,128)} %bitcast.92, f32[2,1,1,8,2,1,256,256]{7,6,4,3,0,5,2,1:T(8,128)} %bitcast.97, f32[]{:T(128)} %bitcast.117, f32[]{:T(128)} %bitcast.116, f32[]{:T(128)} %bitcast.114, f32[]{:T(128)} %bitcast.113, f32[]{:T(128)} %bitcast.112, f32[]{:T(128)} %bitcast.111, ...), kind=kLoop, calls=%fused_computation.58 | loop fusion | flops 7864320 | bytes 18874400 | tf_op jit(solution)/shard_map/sub | solution.py:49
  535.7 11.3 %fusion.28 = f32[1,1,1,8,1,256,256]{6,5,3,0,4,2,1:T(8,128)S(1)} fusion(f32[2,1,1,8,2,1,256,256]{7,6,4,3,0,5,2,1:T(8,128)} %bitcast.92, f32[2,1,1,8,2,1,256,256]{7,6,4,3,0,5,2,1:T(8,128)} %bitcast.97, f32[]{:T(128)} %bitcast.103, f32[]{:T(128)} %bitcast.102, f32[]{:T(128)} %bitcast.100, f32[]{:T(128)} %bitcast.99, f32[]{:T(128)} %bitcast.98, f32[]{:T(128)} %bitcast.95, ...), kind=kLoop, calls=%fused_computation.54 | loop fusion | flops 7864320 | bytes 18874400 | tf_op jit(solution)/shard_map/add | solution.py:50
  547.0 11.3 %fusion.23 = f32[1,1,1,8,1,256,256]{6,5,3,0,4,2,1:T(8,128)S(1)} fusion(f32[2,1,1,8,2,1,256,256]{7,6,4,3,0,5,2,1:T(8,128)} %bitcast.92, f32[2,1,1,8,2,1,256,256]{7,6,4,3,0,5,2,1:T(8,128)} %bitcast.97, f32[]{:T(128)} %bitcast.103, f32[]{:T(128)} %bitcast.102, f32[]{:T(128)} %bitcast.100, f32[]{:T(128)} %bitcast.99, f32[]{:T(128)} %bitcast.98, f32[]{:T(128)} %bitcast.95, ...), kind=kLoop, calls=%fused_computation.49 | loop fusion | flops 7864320 | bytes 18874400 | tf_op jit(solution)/shard_map/sub | solution.py:49
  558.3 0.3 maximum_bitcast_fusion.5
  558.6 0.3 maximum_bitcast_fusion.4
  558.9 0.9 pad_maximum_fusion.3
  559.7 0.9 copy.171
  560.6 4.9 copy.172
  565.5 101.3 %all_to_all.5 = f32[2,1,1,16,256,256]{5,3,0,2,1,4:T(8,128)S(1)} all-to-all(f32[2,1,1,16,256,256]{5,3,0,2,1,4:T(8,128)S(1)} %copy.172), channel_id=1, replica_groups=mesh['wide'=16,'narrow'=8] {'wide'}, dimensions={4} | all-to-all | bytes 16777216 | tf_op jit(solution)/shard_map/all_to_all | solution.py:62
  666.8 8.3 %copy.173 = f32[2,1,1,16,256,256]{5,4,3,2,1,0:T(8,128)} copy(f32[2,1,1,16,256,256]{5,3,0,2,1,4:T(8,128)S(1)} %all_to_all.5) | data formatting | bytes 16777216 | tf_op jit(solution)/shard_map/all_to_all | solution.py:62
  (22 shorter events, 0.0 us)
Async XLA Ops:
  0.0 5.5 copy-start.2
  5.5 4.5 copy-start.10
  10.0 3.5 copy-start.11
  38.3 7.3 %copy-start.1 = (f32[16,256,256]{2,1,0:T(8,128)}, f32[16,256,256]{2,1,0:T(8,128)S(1)}, u32[]{:S(2)}) copy-start(f32[16,256,256]{2,1,0:T(8,128)S(1)} %convolution_add_fusion) | copy-start | bytes 12582916
  45.5 4.5 copy-start
  50.0 22.7 %collective-permute-start = (f32[2,1,1,16,256,256]{4,5,3,2,1,0:T(8,128)}, f32[2,1,1,16,256,256]{4,5,3,2,1,0:T(8,128)}, u32[]{:S(2)}, u32[]{:S(2)}) collective-permute-start(f32[2,1,1,16,256,256]{4,5,3,2,1,0:T(8,128)} %pad_maximum_fusion), channel_id=1, source_target_pairs={{0,8},{8,0},{16,24},{24,16},{32,40},{40,32},{48,56},{56,48},{64,72... | collective-permute-start | bytes 25165832 | tf_op jit(solution)/shard_map/ppermute | solution.py:10
  68.4 2.9 copy-start.12
  91.2 12.4 %copy-start.7 = (f32[1,1,1,8,1,1,256,256]{7,6,3,5,4,2,1,0:T(8,128)S(1)}, f32[1,1,1,8,1,1,256,256]{7,6,3,5,4,2,1,0:T(8,128)}, u32[]{:S(2)}) copy-start(f32[1,1,1,8,1,1,256,256]{7,6,3,5,4,2,1,0:T(8,128)} %copy.187) | copy-start | bytes 6291460
  91.2 12.4 %copy-start.8 = (f32[1,1,1,8,1,1,256,256]{7,6,3,5,4,2,1,0:T(8,128)S(1)}, f32[1,1,1,8,1,1,256,256]{7,6,3,5,4,2,1,0:T(8,128)}, u32[]{:S(2)}) copy-start(f32[1,1,1,8,1,1,256,256]{7,6,3,5,4,2,1,0:T(8,128)} %copy.184) | copy-start | bytes 6291460
  91.2 12.4 %copy-start.9 = (f32[1,1,1,8,1,1,256,256]{7,6,3,5,4,2,1,0:T(8,128)S(1)}, f32[1,1,1,8,1,1,256,256]{7,6,3,5,4,2,1,0:T(8,128)}, u32[]{:S(2)}) copy-start(f32[1,1,1,8,1,1,256,256]{7,6,3,5,4,2,1,0:T(8,128)} %copy.183) | copy-start | bytes 6291460
  103.1 1.6 copy-start.3
  103.1 2.2 copy-start.4
  103.2 2.8 copy-start.5
  103.2 3.4 copy-start.6
  117.9 182.3 %collective-permute-start.1 = (f32[2,1,1,16,256,256]{5,4,3,0,2,1:T(8,128)}, f32[2,1,1,16,256,256]{5,4,3,0,2,1:T(8,128)S(1)}, u32[]{:S(2)}, u32[]{:S(2)}) collective-permute-start(f32[2,1,1,16,256,256]{5,4,3,0,2,1:T(8,128)} %bitcast.372), channel_id=1, source_target_pairs={{0,32},{8,40},{16,48},{24,56},{32,0},{40,8},{48,16},{56,24},{64,96... | collective-permute-start | bytes 25165832 | tf_op jit(solution)/shard_map/ppermute | solution.py:10
  329.7 183.1 %collective-permute-start.2 = (f32[2,1,1,16,256,256]{5,4,3,0,2,1:T(8,128)}, f32[2,1,1,16,256,256]{5,4,3,0,2,1:T(8,128)}, u32[]{:S(2)}, u32[]{:S(2)}) collective-permute-start(f32[2,1,1,16,256,256]{5,4,3,0,2,1:T(8,128)} %bitcast.96), channel_id=1, source_target_pairs={{0,2},{1,3},{2,0},{3,1},{4,6},{5,7},{6,4},{7,5},{8,10},{9,11},{10,... | collective-permute-start | bytes 25165832 | tf_op jit(solution)/shard_map/ppermute | solution.py:10
where the time goes:
time: 686 us; the launch traced here: 675 us
  waiting for transfers between devices  351 us (51%)
  other arithmetic  104 us (15%)
  blocking collectives  101 us (15%)
  local copies, waits for them, and re-layouts  66.9 us (10%)
  matrix products  45.4 us (7%)
    ppermute x3, waiting for transfers between devices, swapped(): lax.ppermute(x, axis, [(i, i ^ 1 << bit) for i in range(lax.axis_size(axi...  351 us
    all_to_all x1, blocking collectives, remap_qubits(): lax.all_to_all(state, 'wide', split_axis=4, concat_axis=4, tiled=True)  101 us
    sub x6, other arithmetic, partner_gate(): total_real + coef_real * amplitude[0] - coef_imag * amplitude[1]  53.5 us
    add x4, other arithmetic, partner_gate(): total_imag + coef_real * amplitude[1] + coef_imag * amplitude[0]  34.9 us
    unnamed x34, local copies, waits for them, and re-layouts  25.4 us
  transfers between devices with their start and end apart: 3, of which 2 were waited for; matrix products, arithmetic and copies ran while one was open for 5% of the time, Pallas kernels for 0%

commit v1 on v0

--- a/solution.py
+++ b/solution.py
@@ -1,9 +1,25 @@
+import functools
 import jax
 import jax.numpy as jnp
 from jax import lax
 from jax.sharding import PartitionSpec as P
 
 highest = lax.Precision.HIGHEST
+
+
+def number_run(mat, chip_axis):
+    return jnp.concatenate(
+        jax.lax.all_to_all(
+            jnp.stack(jnp.split(mat, jax.lax.axis_size(chip_axis), axis=4)),
+            concat_axis=0,
+            axis_name=chip_axis,
+            split_axis=0,
+        ),
+        axis=4,
+    )
+
+
+cut_frame_in = functools.partial(number_run, chip_axis="wide")
 
 
 def swapped(x, axis, bit):
@@ -59,7 +75,7 @@
 
 
 def remap_qubits(state):
-    return lax.all_to_all(state, "wide", split_axis=4, concat_axis=4, tiled=True)
+    return cut_frame_in(state)
 
 
 def body(amplitudes, low_gate, mid_gate, pair_gates):

time: 686 us -> 667 us (0.972)
  local copies, waits for them, and re-layouts: 66.9 us -> 17.6 us
  other arithmetic: 104 us -> 126 us
  waiting for transfers between devices: 351 us -> 362 us
    unnamed x34 -> x31, local copies, waits for them, and re-layouts: 25.4 us -> 0.79 us
    add x4 -> x6, other arithmetic: 34.9 us -> 53.1 us  [partner_gate(): total_imag + coef_real * amplitude[1] + coef_imag * amplitude[0]]
    slice x2 -> x0, local copies, waits for them, and re-layouts: 11.5 us -> none  [partner_gate(): amplitude[1]]
    ppermute x3, waiting for transfers between devices: 351 us -> 362 us  [swapped(): lax.ppermute(x, axis, [(i, i ^ 1 << bit) for i in range(lax.axis_size(axi...]
    all_to_all x1 -> x0, local copies, waits for them, and re-layouts: 8.25 us -> none  [remap_qubits(): lax.all_to_all(state, 'wide', split_axis=4, concat_axis=4, tiled=True)]
  transfers between devices with their start and end apart: 3 -> 3, of which waited for: 2 -> 3; matrix products, arithmetic and copies ran while one was open for 5% -> 2% of each run, Pallas kernels for 0% -> 0%
where the time goes in v1:
time: 667 us; the launch traced here: 656 us
  waiting for transfers between devices  362 us (54%)
  other arithmetic  126 us (19%)
  blocking collectives  101 us (15%)
  matrix products  43.1 us (6%)
  local copies, waits for them, and re-layouts  17.6 us (3%)
    ppermute x3, waiting for transfers between devices, swapped(): lax.ppermute(x, axis, [(i, i ^ 1 << bit) for i in range(lax.axis_size(axi...  362 us
    all_to_all x1, blocking collectives, number_run(): jax.lax.all_to_all(jnp.stack(jnp.split(mat, jax.lax.axis_size(chip_axis),...  101 us
    sub x6, other arithmetic, partner_gate(): total_real + coef_real * amplitude[0] - coef_imag * amplitude[1]  56.6 us
    add x6, other arithmetic, partner_gate(): total_imag + coef_real * amplitude[1] + coef_imag * amplitude[0]  53.1 us
  transfers between devices with their start and end apart: 3, of which 3 were waited for; matrix products, arithmetic and copies ran while one was open for 2% of the time, Pallas kernels for 0%

profile of v1, /device:TPU:1, one launch (start us, length us, event | category | flops | bytes accessed | tf_op | source)
XLA Modules:
  0.0 656.3 jit_solution(12506741555727102593)
XLA Ops:
  0.0 0.0 copy-start.4
  0.0 5.5 fusion.2
  5.5 0.0 copy-done.4
  5.5 0.0 copy-start.5
  5.5 4.5 fusion
  10.0 0.0 copy-done.5
  10.0 0.0 copy-start.6
  10.0 3.5 fusion.12
  13.5 0.0 copy-done.6
  13.5 4.3 fusion.62
  17.8 12.8 %fusion.58 = f32[16,256,256]{1,2,0:T(8,128)S(1)} fusion(f32[16,256,256]{2,1,0:T(8,128)S(1)} %fusion.12, f32[2,256,256]{2,1,0:T(8,128)S(1)} %copy-done.6), kind=kOutput, calls=%fused_computation.117 | convolution fusion | flops 3221225472 | bytes 8650752 | tf_op jit(solution)/shard_map/abhml,im->abhil/dot_general | solution.py:42
  30.6 3.6 fusion.15
  34.2 4.4 convolution_subtract_fusion
  38.6 0.0 copy-start
  38.6 4.6 convolution_add_fusion
  43.2 0.0 copy-start.2
  43.3 0.0 copy-done
  43.3 0.0 copy-start.7
  43.3 4.3 pad_maximum_fusion
  47.6 0.1 copy-done.2
  47.7 1.4 collective-permute-start
  49.1 0.0 copy-done.7
  49.1 0.1 dynamic-slice_bitcast_fusion.3
  49.2 0.7 fusion.82
  49.9 0.7 fusion.83
  50.6 11.7 %collective-permute-done = f32[2,1,1,16,256,256]{5,4,3,2,1,0:T(8,128)} collective-permute-done((f32[2,1,1,16,256,256]{5,4,3,2,1,0:T(8,128)}, f32[2,1,1,16,256,256]{5,4,3,2,1,0:T(8,128)}, u32[]{:S(2)}, u32[]{:S(2)}) %collective-permute-start) | collective-permute-done | bytes 8388640 | tf_op jit(solution)/shard_map/ppermute | solution.py:26
  62.3 0.0 copy-start.1
  62.3 12.6 %add_subtract_fusion.1 = f32[1,1,1,8,1,1,256,256]{7,6,3,5,4,2,1,0:T(8,128)S(1)} fusion(f32[1,1,1,8,2,1,256,256]{7,6,4,3,5,2,1,0:T(8,128)} %bitcast.504, f32[1,1,1,8,2,1,256,256]{7,6,4,3,5,2,1,0:T(8,128)} %bitcast.509, f32[2,1,1,8,2,1,256,256]{7,6,4,3,0,5,2,1:T(8,128)} %bitcast.33, f32[]{:T(128)} %bitcast.40, f32[]{:T(128)} %bitcast.39, f32[]{:T(128)} %bitcast.37, ...), kind=kLoop, calls=%fused_computation.84 | loop fusion | flops 7864320 | bytes 18874400 | tf_op jit(solution)/shard_map/sub | solution.py:65
  74.8 0.0 copy-done.1
  74.9 0.0 copy-done.3
  74.9 9.1 %add_add_fusion.1 = f32[1,1,1,8,1,1,256,256]{7,6,3,5,4,2,1,0:T(8,128)S(1)} fusion(f32[1,1,1,8,2,1,256,256]{7,6,4,3,5,2,1,0:T(8,128)S(1)} %bitcast.505, f32[1,1,1,8,2,1,256,256]{7,6,4,3,5,2,1,0:T(8,128)S(1)} %bitcast.510, f32[2,1,1,8,2,1,256,256]{7,6,4,3,0,5,2,1:T(8,128)} %bitcast.33, f32[]{:T(128)} %bitcast.40, f32[]{:T(128)} %bitcast.39, f32[]{:T(128)} %bitcast.37, ...), kind=kLoop, calls=%fused_computation.83 | loop fusion | flops 7864320 | bytes 18874400 | tf_op jit(solution)/shard_map/add | solution.py:66
  84.0 9.0 %add_subtract_fusion = f32[1,1,1,8,1,1,256,256]{7,6,3,5,4,2,1,0:T(8,128)S(1)} fusion(f32[1,1,1,8,2,1,256,256]{7,6,4,3,5,2,1,0:T(8,128)S(1)} %bitcast.506, f32[1,1,1,8,2,1,256,256]{7,6,4,3,5,2,1,0:T(8,128)S(1)} %bitcast.511, f32[2,1,1,8,2,1,256,256]{7,6,4,3,0,5,2,1:T(8,128)} %bitcast.33, f32[]{:T(128)} %bitcast.50, f32[]{:T(128)} %bitcast.49, f32[]{:T(128)} %bitcast.48, ...), kind=kLoop, calls=%fused_computation.82 | loop fusion | flops 7864320 | bytes 18874400 | tf_op jit(solution)/shard_map/sub | solution.py:65
  93.0 9.0 %add_add_fusion = f32[1,1,1,8,1,1,256,256]{7,6,3,5,4,2,1,0:T(8,128)S(1)} fusion(f32[1,1,1,8,2,1,256,256]{7,6,4,3,5,2,1,0:T(8,128)S(1)} %bitcast.507, f32[1,1,1,8,2,1,256,256]{7,6,4,3,5,2,1,0:T(8,128)S(1)} %bitcast.512, f32[2,1,1,8,2,1,256,256]{7,6,4,3,0,5,2,1:T(8,128)} %bitcast.33, f32[]{:T(128)} %bitcast.50, f32[]{:T(128)} %bitcast.49, f32[]{:T(128)} %bitcast.48, ...), kind=kLoop, calls=%fused_computation.81 | loop fusion | flops 7864320 | bytes 18874400 | tf_op jit(solution)/shard_map/add | solution.py:66
  102.0 0.4 maximum_bitcast_fusion
  102.4 0.4 maximum_bitcast_fusion.1
  102.8 4.0 pad_maximum_fusion.1
  106.8 1.3 collective-permute-start.1
  108.1 0.7 fusion.80
  108.7 0.6 fusion.81
  109.4 3.9 maximum_maximum_fusion
  113.2 4.0 fusion.76
  117.3 171.4 %collective-permute-done.1 = f32[2,1,1,16,256,256]{5,4,3,0,2,1:T(8,128)S(1)} collective-permute-done((f32[2,1,1,16,256,256]{5,4,3,0,2,1:T(8,128)}, f32[2,1,1,16,256,256]{5,4,3,0,2,1:T(8,128)S(1)}, u32[]{:S(2)}, u32[]{:S(2)}) %collective-permute-start.1) | collective-permute-done | bytes 8388640 | tf_op jit(solution)/shard_map/ppermute | solution.py:26
  288.6 6.1 fusion.36
  294.8 6.1 fusion.39
  300.9 6.1 fusion.41
  307.0 6.1 fusion.33
  313.1 0.3 maximum_bitcast_fusion.2
  313.4 0.3 maximum_bitcast_fusion.3
  313.7 0.9 pad_maximum_fusion.2
  314.6 4.0 copy.172
  318.6 3.0 collective-permute-start.2
  321.6 0.1 dynamic-slice_bitcast_fusion.5
  321.6 0.7 fusion.78
  322.3 178.9 %collective-permute-done.2 = f32[2,1,1,16,256,256]{5,4,3,0,2,1:T(8,128)} collective-permute-done((f32[2,1,1,16,256,256]{5,4,3,0,2,1:T(8,128)}, f32[2,1,1,16,256,256]{5,4,3,0,2,1:T(8,128)}, u32[]{:S(2)}, u32[]{:S(2)}) %collective-permute-start.2) | collective-permute-done | bytes 8388640 | tf_op jit(solution)/shard_map/ppermute | solution.py:26
  501.2 11.4 %fusion.23 = f32[1,1,1,8,1,256,256]{6,5,3,0,4,2,1:T(8,128)S(1)} fusion(f32[2,1,1,8,2,1,256,256]{7,6,4,3,0,5,2,1:T(8,128)} %bitcast.92, f32[2,1,1,8,2,1,256,256]{7,6,4,3,0,5,2,1:T(8,128)} %bitcast.97, f32[]{:T(128)} %bitcast.103, f32[]{:T(128)} %bitcast.102, f32[]{:T(128)} %bitcast.100, f32[]{:T(128)} %bitcast.99, f32[]{:T(128)} %bitcast.98, f32[]{:T(128)} %bitcast.95, ...), kind=kLoop, calls=%fused_computation.57 | loop fusion | flops 7864320 | bytes 18874400 | tf_op jit(solution)/shard_map/sub | solution.py:65
  512.6 11.4 %fusion.28 = f32[1,1,1,8,1,256,256]{6,5,3,0,4,2,1:T(8,128)S(1)} fusion(f32[2,1,1,8,2,1,256,256]{7,6,4,3,0,5,2,1:T(8,128)} %bitcast.92, f32[2,1,1,8,2,1,256,256]{7,6,4,3,0,5,2,1:T(8,128)} %bitcast.97, f32[]{:T(128)} %bitcast.103, f32[]{:T(128)} %bitcast.102, f32[]{:T(128)} %bitcast.100, f32[]{:T(128)} %bitcast.99, f32[]{:T(128)} %bitcast.98, f32[]{:T(128)} %bitcast.95, ...), kind=kLoop, calls=%fused_computation.62 | loop fusion | flops 7864320 | bytes 18874400 | tf_op jit(solution)/shard_map/add | solution.py:66
  524.0 11.4 %fusion.32 = f32[1,1,1,8,1,256,256]{6,5,3,4,2,1,0:T(8,128)S(1)} fusion(f32[2,1,1,8,2,1,256,256]{7,6,4,3,0,5,2,1:T(8,128)} %bitcast.92, f32[2,1,1,8,2,1,256,256]{7,6,4,3,0,5,2,1:T(8,128)} %bitcast.97, f32[]{:T(128)} %bitcast.117, f32[]{:T(128)} %bitcast.116, f32[]{:T(128)} %bitcast.114, f32[]{:T(128)} %bitcast.113, f32[]{:T(128)} %bitcast.112, f32[]{:T(128)} %bitcast.111, ...), kind=kLoop, calls=%fused_computation.66 | loop fusion | flops 7864320 | bytes 18874400 | tf_op jit(solution)/shard_map/sub | solution.py:65
  535.4 11.4 %fusion.18 = f32[1,1,1,8,1,256,256]{6,5,3,4,2,1,0:T(8,128)S(1)} fusion(f32[2,1,1,8,2,1,256,256]{7,6,4,3,0,5,2,1:T(8,128)} %bitcast.92, f32[2,1,1,8,2,1,256,256]{7,6,4,3,0,5,2,1:T(8,128)} %bitcast.97, f32[]{:T(128)} %bitcast.117, f32[]{:T(128)} %bitcast.116, f32[]{:T(128)} %bitcast.114, f32[]{:T(128)} %bitcast.113, f32[]{:T(128)} %bitcast.112, f32[]{:T(128)} %bitcast.111, ...), kind=kLoop, calls=%fused_computation.46 | loop fusion | flops 7864320 | bytes 18874400 | tf_op jit(solution)/shard_map/add | solution.py:66
  546.8 0.3 maximum_bitcast_fusion.4
  547.1 0.3 maximum_bitcast_fusion.5
  547.4 0.9 pad_maximum_fusion.3
  548.3 0.9 copy.190
  549.9 101.5 %all_to_all.5 = f32[16,2,1,1,16,16,256]{6,5,4,1,3,2,0:T(8,128)S(1)} all-to-all(f32[16,2,1,1,16,16,256]{6,5,4,1,3,2,0:T(8,128)S(1)} %fusion.42), channel_id=1, replica_groups=mesh['wide'=16,'narrow'=8] {'wide'}, dimensions={0} | all-to-all | bytes 16777216 | tf_op jit(solution)/shard_map/all_to_all | solution.py:12
  651.4 4.4 copy.191
  (18 shorter events, 0.7 us)
Async XLA Ops:
  0.0 5.5 copy-start.4
  5.5 4.5 copy-start.5
  10.0 3.5 copy-start.6
  38.6 4.6 copy-start
  43.2 4.5 copy-start.2
  43.3 5.9 copy-start.7
  47.7 14.5 %collective-permute-start = (f32[2,1,1,16,256,256]{5,4,3,2,1,0:T(8,128)}, f32[2,1,1,16,256,256]{5,4,3,2,1,0:T(8,128)}, u32[]{:S(2)}, u32[]{:S(2)}) collective-permute-start(f32[2,1,1,16,256,256]{5,4,3,2,1,0:T(8,128)} %pad_maximum_fusion), channel_id=1, source_target_pairs={{0,8},{8,0},{16,24},{24,16},{32,40},{40,32},{48,56},{56,48},{64,72... | collective-permute-start | bytes 25165832 | tf_op jit(solution)/shard_map/ppermute | solution.py:26
  62.3 12.6 %copy-start.1 = (f32[16,256,256]{1,2,0:T(8,128)S(1)}, f32[16,256,256]{1,2,0:T(8,128)}, u32[]{:S(2)}) copy-start(f32[16,256,256]{1,2,0:T(8,128)} %copy-done) | copy-start | bytes 12582916
  62.3 12.6 %copy-start.3 = (f32[16,256,256]{1,2,0:T(8,128)S(1)}, f32[16,256,256]{1,2,0:T(8,128)}, u32[]{:S(2)}) copy-start(f32[16,256,256]{1,2,0:T(8,128)} %copy-done.2) | copy-start | bytes 12582916
  106.8 181.9 %collective-permute-start.1 = (f32[2,1,1,16,256,256]{5,4,3,0,2,1:T(8,128)}, f32[2,1,1,16,256,256]{5,4,3,0,2,1:T(8,128)S(1)}, u32[]{:S(2)}, u32[]{:S(2)}) collective-permute-start(f32[2,1,1,16,256,256]{5,4,3,0,2,1:T(8,128)} %bitcast.542), channel_id=1, source_target_pairs={{0,32},{8,40},{16,48},{24,56},{32,0},{40,8},{48,16},{56,24},{64,96... | collective-permute-start | bytes 25165832 | tf_op jit(solution)/shard_map/ppermute | solution.py:26
  318.6 182.6 %collective-permute-start.2 = (f32[2,1,1,16,256,256]{5,4,3,0,2,1:T(8,128)}, f32[2,1,1,16,256,256]{5,4,3,0,2,1:T(8,128)}, u32[]{:S(2)}, u32[]{:S(2)}) collective-permute-start(f32[2,1,1,16,256,256]{5,4,3,0,2,1:T(8,128)} %bitcast.96), channel_id=1, source_target_pairs={{0,2},{1,3},{2,0},{3,1},{4,6},{5,7},{6,4},{7,5},{8,10},{9,11},{10,... | collective-permute-start | bytes 25165832 | tf_op jit(solution)/shard_map/ppermute | solution.py:26
